TPU v7x, 128 devices: a whole 4x4x4 slice. The times are simulated.
128 devices in a mesh: sky: 16 (over x, z), depth: 8 (over y, core).
Axes of the slice: x: 4, y: 4, z: 4, core: 2. Of those that a mesh axis runs over, the one named last changes fastest.
Arguments:
- positions: float32 [3, 2048, 128], P(None, ('sky', 'depth')), may hold values from 0 to 1
- cell_points: int32 [2048], P(('sky', 'depth')), may hold values from 1 to 128
- target_log: float32 [16], replicated, may hold values from 8 to 20
- export_count: int32 [128, 128], P(('sky', 'depth')), may hold values from 0 to 3, as said below
- export_cell: int32 [128, 128, 3], P(('sky', 'depth')), may hold values from 0 to 15
- import_pair: int32 [128, 128, 3], P(('sky', 'depth')), may hold values from 0 to 15
- import_shift: int32 [3, 128, 128, 3], P(None, ('sky', 'depth')), may hold values from -1 to 1, as said below
Outputs:
- travel: float32 [3, 2048, 128], P(None, ('sky', 'depth'))
Inputs may be any that keep to these rules, and one draw needn't show every extreme that they name: export_count[s, t] counts the slots of export_cell[s, t] that are used; it is zero unless s and t are distinct devices whose sky indices differ by at most one modulo the sky axis's size and whose depth indices differ by at most one; in every draw some device t receives 3 cells from each such neighbour. For neighbouring devices t and s, components 0 and 2 of import_shift[:, t, s, k] are the sky step and the depth step from t's region to s's region (sky taken around the cycle), component 1 varies; all components are zero for devices that are not neighbours.
All inputs are finite; a program needn't handle non-finite values.
Results may differ from a plain program's by a relative error of at most 0.00022.
Values sent between devices are 32-bit elements; how exact they have to be, the bound alone decides.
No kernel may reach another device: no remote copies, remote signals or barrier semaphores. Data moves between devices by JAX's collectives and lax.ppermute only.
A program may use at most 64 MiB of HBM per device.

v0:
```python
import functools
import math

import jax
import jax.numpy as jnp
from jax import lax
from jax.experimental import pallas as pl
from jax.experimental.pallas import tpu as pltpu
from jax.sharding import PartitionSpec as P

STEPS = 2
EPS_SQ = 0.0001
STEP_SIZE = 0.01

BINS = 16
CELLS = 16
POINTS = 128
SLOTS = 3
AXES = ("sky", "depth")

UNIT = math.sqrt(128.0 * math.log2(math.e))
CENTRES = [(b + 0.5) / 16.0 for b in range(BINS)]
CHAIN = 4
LIFT = 64.0
MIDDLE = CENTRES[8]
RADIUS_CAP = 2.1 * UNIT
FAR = 1.0e4
COUNT_SCALE = [
    math.exp(16.0 * (b % CHAIN) * (MIDDLE - CENTRES[b - b % CHAIN]) - 0.5 * (b % CHAIN) ** 2) * 2.0**-LIFT
    for b in range(BINS)
]
FORCE_SCALE = [-256.0 / UNIT * scale for scale in COUNT_SCALE]

NEIGHBOURS = [(0, 1), (0, 2), (1, 0), (1, 1), (1, 2), (2, 0), (2, 1), (2, 2)]
TABLE_ROW = 16
EXPORT, IMPORT, LIVE, SHIFT = 0, SLOTS, 2 * SLOTS, 2 * SLOTS + 1
SIZES = len(NEIGHBOURS) * TABLE_ROW
TABLE = SIZES + CELLS
STEP_ROWS = 16
BLOCKS = POINTS // STEP_ROWS
UNROLL = 4

VMEM = pl.BlockSpec(memory_space=pltpu.VMEM)
SMEM = pl.BlockSpec(memory_space=pltpu.SMEM)
PARAMS = pltpu.CompilerParams(vmem_limit_bytes=40 * 1024 * 1024)


def partner(axis, option):
    here = lax.axis_index(axis)
    if option == 0:
        return here
    step = 1 - 2 * (here % 2)
    return here + step if option == 1 else here - step


def neighbour(sky_option, depth_option):
    sky_count, depth_count = lax.axis_size("sky"), lax.axis_size("depth")
    sky = lax.rem(partner("sky", sky_option) + sky_count, sky_count)
    depth = partner("depth", depth_option)
    inside = (depth >= 0) & (depth < depth_count)
    return sky * depth_count + jnp.clip(depth, 0, depth_count - 1), inside


def column(values, shape):
    rows = lax.broadcasted_iota(jnp.int32, shape, 0)
    out = jnp.full(shape, values[0], jnp.float32)
    for index in range(1, len(values)):
        out = jnp.where(rows == index, values[index], out)
    return out


def shift_of(table, index, slot):
    rows = lax.broadcasted_iota(jnp.int32, (4, POINTS), 0)
    shift = jnp.zeros((4, POINTS), jnp.float32)
    for axis in range(3):
        amount = table[index * TABLE_ROW + SHIFT + axis * SLOTS + slot].astype(jnp.float32) * UNIT
        shift = jnp.where(rows == axis, amount, shift)
    return shift


def pack(source, table, outs):
    depth_even, depth_odd, sky_even, sky_odd = outs
    lanes = lax.broadcasted_iota(jnp.int32, (4, POINTS), 1)
    for index, (sky_option, depth_option) in enumerate(NEIGHBOURS):
        if depth_option == 0:
            out = sky_even if sky_option == 1 else sky_odd
        else:
            out = (depth_even if depth_option == 1 else depth_odd).at[sky_option]
        row = index * TABLE_ROW
        live = table[row + LIVE]
        meta = jnp.zeros((4, POINTS), jnp.float32)
        for slot in range(SLOTS):
            right = table[row + EXPORT + slot]
            out[slot] = source[right]
            size = jnp.where(slot < live, table[SIZES + right], 0)
            meta = jnp.where(lanes == slot, size.astype(jnp.float32), meta)
            left = table[row + IMPORT + slot]
            out[SLOTS + slot] = source[left] - shift_of(table, index, slot)
            size = table[SIZES + left]
            meta = jnp.where(lanes == SLOTS + slot, size.astype(jnp.float32), meta)
        out[2 * SLOTS] = meta


def first_kernel(
    positions_in, points_in, logs_in, count_in, export_in, import_in, shift_in,
    target, logs, table, depth_even, depth_odd, sky_even, sky_odd,
    positions, points, log_list, count, exports, imports, shifts, source, sems,
):
    pairs = [
        (points_in, points), (count_in, count), (export_in, exports), (import_in, imports),
        (shift_in, shifts), (positions_in, positions), (logs_in, log_list),
    ]
    copies = [
        pltpu.make_async_copy(origin, place, sems.at[index])
        for index, (origin, place) in enumerate(pairs)
    ]
    for copy in copies:
        copy.start()
    for copy in copies:
        copy.wait()
    for cell in range(CELLS):
        table[SIZES + cell] = points[cell]
    for index, options in enumerate(NEIGHBOURS):
        device, inside = neighbour(*options)
        row = index * TABLE_ROW
        table[row + LIVE] = jnp.where(inside, count[0, device], 0)
        for slot in range(SLOTS):
            table[row + EXPORT + slot] = exports[slot, 0, device]
            table[row + IMPORT + slot] = imports[slot, 0, device]
            for axis in range(3):
                table[row + SHIFT + axis * SLOTS + slot] = shifts[axis, slot, 0, device]
    logs[...] = column([log_list[b] for b in range(BINS)], (BINS, POINTS))
    lanes = lax.broadcasted_iota(jnp.int32, (4, POINTS), 1)
    for cell in range(CELLS):
        rows = [positions[axis, cell : cell + 1, :] for axis in range(3)]
        tile = jnp.concatenate(rows + [jnp.zeros((1, POINTS), jnp.float32)], axis=0) * UNIT
        live = lanes < points[cell]
        target[cell] = jnp.where(live, tile, -FAR)
        source[cell] = jnp.where(live, tile, FAR)
    pack(source, table, (depth_even, depth_odd, sky_even, sky_odd))


def shape_pairs(at, row_list, cell_list, source, base, target):
    units = range(UNROLL)
    blocks = [
        source[pl.ds(pl.multiple_of(row_list[at + unit] * STEP_ROWS, STEP_ROWS), STEP_ROWS), :]
        for unit in units
    ]
    spread = [
        [
            jnp.broadcast_to(blocks[unit][:, base + axis : base + axis + 1], (STEP_ROWS, POINTS))
            for unit in units
        ]
        for axis in range(3)
    ]
    out = []
    for unit in units:
        cell = cell_list[at + unit]
        dx, dy, dz = (target[cell, axis : axis + 1, :] - spread[axis][unit] for axis in range(3))
        square = dx * dx + dy * dy + dz * dz + EPS_SQ * UNIT * UNIT
        inverse = lax.rsqrt(square)
        radius = jnp.minimum(square * inverse, RADIUS_CAP)
        ratio = jnp.exp2(
            radius * (16.0 * math.log2(math.e) / UNIT) - 16.0 * math.log2(math.e) * MIDDLE
        )
        out.append((radius, ratio, dx * inverse, dy * inverse, dz * inverse))
    return out


def add_block(values, cell, force, counts):
    radius, ratio, *units = values
    for chain in range(BINS // CHAIN):
        for link in range(CHAIN):
            b = chain * CHAIN + link
            delta = radius - CENTRES[b] * UNIT
            if link == 0:
                value = jnp.exp2(LIFT - delta * delta)
            else:
                value = value * ratio
            if counts is not None:
                counts[b] += value[:8] + value[8:]
            slope = value * delta
            for axis in range(3):
                pulled = slope * units[axis]
                force[cell, axis * BINS + b] += pulled[:8] + pulled[8:]


def add_blocks(total, row_list, cell_list, base, target, source, force, counts):
    def step(turn, shapes):
        at = turn * UNROLL
        ahead = shape_pairs(at + UNROLL, row_list, cell_list, source, base, target)
        for unit in range(UNROLL):
            add_block(shapes[unit], cell_list[at + unit], force, counts)
        return ahead

    first = shape_pairs(0, row_list, cell_list, source, base, target)
    lax.fori_loop(0, (total + (UNROLL - 1)) // UNROLL, step, first)


def list_blocks(at, slot, cell, size, row_list, cell_list):
    for block in range(BLOCKS):
        row_list[at + block] = slot * BLOCKS + block
        cell_list[at + block] = cell
    return at + (size + (STEP_ROWS - 1)) // STEP_ROWS


def end_list(at, slots, row_list, cell_list):
    for spare in range(3 * UNROLL):
        row_list[at + spare] = slots * BLOCKS
        cell_list[at + spare] = 0


def put_points(source, slot, first, second):
    source[slot * POINTS : (slot + 1) * POINTS] = jnp.transpose(
        jnp.concatenate([first, second], axis=0), (1, 0)
    )


def self_kernel(target, table, force, counts, source, row_list, cell_list):
    lanes = lax.broadcasted_iota(jnp.int32, (4, POINTS), 1)
    end = 0
    for cell in range(CELLS):
        size = table[SIZES + cell]
        tile = jnp.where(lanes < size, target[cell], FAR)
        put_points(source, cell, tile, tile)
        end = list_blocks(end, cell, cell, size, row_list, cell_list)
    end_list(end, CELLS, row_list, cell_list)
    source[CELLS * POINTS :] = jnp.full((STEP_ROWS, 8), FAR, jnp.float32)
    force[...] = jnp.zeros(force.shape, jnp.float32)
    counts[...] = jnp.zeros(counts.shape, jnp.float32)
    add_blocks(end, row_list, cell_list, 0, target, source, force, counts)
    counts[...] = 0.5 * counts[...]


def ghost_pairs(
    messages, metas, first, target, table, force, counts,
    source, import_rows, import_cells, export_rows, export_cells, meta, sems,
):
    copies = []
    at = 0
    for index, part in enumerate(metas):
        size = part.shape[0]
        copies.append(pltpu.make_async_copy(part, meta.at[at : at + size], sems.at[index]))
        at += size
    for copy in copies:
        copy.start()
    for index, message in enumerate(messages):
        for slot in range(SLOTS):
            put_points(
                source, index * SLOTS + slot,
                message[slot] + shift_of(table, first + index, slot), message[SLOTS + slot],
            )
    slots = len(messages) * SLOTS
    source[slots * POINTS :] = jnp.full((STEP_ROWS, 8), FAR, jnp.float32)
    for copy in copies:
        copy.wait()
    import_end = 0
    export_end = 0
    for index in range(len(messages)):
        row = (first + index) * TABLE_ROW
        live = table[row + LIVE]
        for slot in range(SLOTS):
            at = index * SLOTS + slot
            size = meta[index, 0, slot].astype(jnp.int32)
            import_end = list_blocks(
                import_end, at, table[row + IMPORT + slot], size, import_rows, import_cells
            )
            size = jnp.where(slot < live, meta[index, 0, SLOTS + slot].astype(jnp.int32), 0)
            export_end = list_blocks(
                export_end, at, table[row + EXPORT + slot], size, export_rows, export_cells
            )
    end_list(import_end, slots, import_rows, import_cells)
    end_list(export_end, slots, export_rows, export_cells)
    add_blocks(
        import_end, import_rows, import_cells, 0, target, source, force, counts
    )
    add_blocks(
        export_end, export_rows, export_cells, 4, target, source, force, None
    )


def near_kernel(target, table, from_even, from_odd, force_in, counts_in, force, counts, *scratch):
    ghost_pairs(
        [from_even.at[0], from_odd.at[0]],
        [side.at[0:1, 2 * SLOTS] for side in (from_even, from_odd)],
        0, target, table, force, counts, *scratch,
    )


def far_kernel(
    target, table, from_even, from_odd, force_in, counts_in, force, counts, grad, payload, *scratch,
):
    ghost_pairs(
        [side.at[index] for side in (from_even, from_odd) for index in range(3)],
        [side.at[:, 2 * SLOTS] for side in (from_even, from_odd)],
        2, target, table, force, counts, *scratch,
    )
    force_scale = column(FORCE_SCALE, (BINS, POINTS))
    for cell in range(CELLS):
        for axis in range(3):
            tile = jnp.sum(force[cell, axis * BINS : (axis + 1) * BINS], axis=1) * force_scale
            at = (cell * 3 + axis) * POINTS
            grad[:, at : at + POINTS] = tile
    whole = grad[...]
    gram = lax.dot_general(
        whole, whole, (((1,), (1,)), ((), ())),
        precision=lax.Precision.HIGHEST, preferred_element_type=jnp.float32,
    )
    bins = lax.broadcasted_iota(jnp.int32, (BINS, POINTS), 0)
    lane = lax.broadcasted_iota(jnp.int32, (BINS, POINTS), 1)
    low, high = lane % BINS, lane // BINS
    spread = jnp.where(low == bins, 1.0, 0.0)
    wide = lax.dot_general(
        gram, spread, (((1,), (0,)), ((), ())),
        precision=lax.Precision.HIGHEST, preferred_element_type=jnp.float32,
    )
    first = jnp.sum(jnp.where(bins == (low + high) % BINS, wide, 0.0), axis=0, keepdims=True)
    second = jnp.where((bins == (low + 8) % BINS) & (high == 0), wide, 0.0)
    sums = jnp.sum(counts[...], axis=1)
    sums = jnp.sum(sums, axis=1, keepdims=True) * column(COUNT_SCALE, (BINS, POINTS))
    second = second + jnp.where(lane == bins + BINS, sums, 0.0)
    total = table[SIZES]
    for cell in range(1, CELLS):
        total = total + table[SIZES + cell]
    second = second + jnp.where((lane == 2 * BINS) & (bins == 0), total.astype(jnp.float32), 0.0)
    second = jnp.sum(second, axis=0, keepdims=True)
    both = jnp.concatenate([first, second], axis=0)
    payload[...] = jnp.broadcast_to(both[None], payload.shape)


def moves_of(sums, grad, logs):
    both = jnp.sum(sums[...], axis=0)
    bins = lax.broadcasted_iota(jnp.int32, (BINS, POINTS), 0)
    lane = lax.broadcasted_iota(jnp.int32, (BINS, POINTS), 1)
    low, high = lane % BINS, lane // BINS
    first, second = both[0:1], both[1:2]
    counts = jnp.sum(
        jnp.where(lane == bins + BINS, jnp.broadcast_to(second, (BINS, POINTS)), 0.0), axis=1, keepdims=True
    )
    counts = jnp.broadcast_to(counts, (BINS, POINTS))
    one_lane = lax.broadcasted_iota(jnp.int32, (1, POINTS), 1)
    valid = jnp.sum(jnp.where(one_lane == 2 * BINS, second, 0.0), axis=1, keepdims=True)
    mean_count = jnp.sum(counts, axis=0, keepdims=True) / BINS
    pull = (jnp.log(1.0 + counts) - logs[...]) * mean_count / (1.0 + counts)
    here = jnp.sum(jnp.where(bins == low, pull, 0.0), axis=0, keepdims=True)
    there = jnp.sum(jnp.where(bins == (low + high) % BINS, pull, 0.0), axis=0, keepdims=True)
    across = jnp.sum(jnp.where(bins == (low + 8) % BINS, pull, 0.0), axis=0, keepdims=True)
    power = first * here * there * jnp.where(one_lane < BINS, 1.0, 2.0)
    power = power + jnp.where(one_lane < BINS, second * here * across, 0.0)
    power = jnp.maximum(jnp.sum(power, axis=1, keepdims=True), 0.0)
    rms = jnp.sqrt(power / (3.0 * valid) + 1e-06)
    weights = pull / -rms
    out = []
    for cell in range(CELLS):
        parts = []
        for axis in range(3):
            at = (cell * 3 + axis) * POINTS
            parts.append(jnp.sum(grad[:, at : at + POINTS] * weights, axis=0, keepdims=True))
        out.append(parts)
    return out


def update_kernel(
    sums, grad, target, logs, table,
    travel, next_target, depth_even, depth_odd, sky_even, sky_odd, source,
):
    lanes = lax.broadcasted_iota(jnp.int32, (4, POINTS), 1)
    moves = moves_of(sums, grad, logs)
    for cell in range(CELLS):
        tile = jnp.concatenate(moves[cell] + [jnp.zeros((1, POINTS), jnp.float32)], axis=0)
        travel[cell] = tile
        tile = target[cell] + (STEP_SIZE * UNIT) * tile
        next_target[cell] = tile
        source[cell] = jnp.where(lanes < table[SIZES + cell], tile, FAR)
    pack(source, table, (depth_even, depth_odd, sky_even, sky_odd))


def last_kernel(sums, grad, travel, logs, out):
    moves = moves_of(sums, grad, logs)
    for cell in range(CELLS):
        for axis in range(3):
            out[axis, cell : cell + 1, :] = travel[cell, axis : axis + 1, :] + moves[cell][axis]


def f32(*shape):
    return jax.ShapeDtypeStruct(shape, jnp.float32)


CELL_SHAPE = (CELLS, 4, POINTS)
GRAD_SHAPE = (BINS, CELLS * 3 * POINTS)
MESSAGE = (2 * SLOTS + 1, 4, POINTS)
MESSAGES = [f32(3, *MESSAGE), f32(3, *MESSAGE), f32(*MESSAGE), f32(*MESSAGE)]


def swap(value, axis, option):
    count = lax.axis_size(axis)
    perm = []
    for low in range(option - 1, count, 2):
        high = low + 1
        if high < count or axis == "sky":
            perm += [(low, high % count), (high % count, low)]
    return lax.ppermute(value, axis, perm)


FORCE_SHAPE = (CELLS, 3 * BINS, 8, POINTS)
COUNT_SHAPE = (BINS, 8, POINTS)


def list_space(slots):
    return pltpu.SMEM((slots * BLOCKS + BLOCKS + 3 * UNROLL,), jnp.int32)


def ghost_space(messages):
    slots = messages * SLOTS
    return (
        [pltpu.VMEM((slots * POINTS + STEP_ROWS, 8), jnp.float32)]
        + [list_space(slots)] * 4
        + [pltpu.SMEM((messages, 4, POINTS), jnp.float32), pltpu.SemaphoreType.DMA((2,))]
    )


def cost(microseconds):
    return pl.CostEstimate(flops=0, transcendentals=0, bytes_accessed=int(microseconds * 3.0e6))


def self_pairs(target, table):
    return pl.pallas_call(
        self_kernel,
        out_shape=[f32(*FORCE_SHAPE), f32(*COUNT_SHAPE)],
        in_specs=[VMEM, SMEM],
        out_specs=[VMEM] * 2,
        scratch_shapes=[pltpu.VMEM((CELLS * POINTS + STEP_ROWS, 8), jnp.float32)]
        + [list_space(CELLS)] * 2,
        compiler_params=PARAMS,
        cost_estimate=cost(6),
        name="self",
    )(target, table)


def near_pairs(target, table, from_even, from_odd, force, counts):
    return pl.pallas_call(
        near_kernel,
        out_shape=[f32(*FORCE_SHAPE), f32(*COUNT_SHAPE)],
        in_specs=[VMEM, SMEM] + [VMEM] * 4,
        out_specs=[VMEM] * 2,
        scratch_shapes=ghost_space(2),
        input_output_aliases={4: 0, 5: 1},
        compiler_params=PARAMS,
        cost_estimate=cost(4),
        name="near",
    )(target, table, from_even, from_odd, force, counts)


def far_pairs(devices, target, table, from_even, from_odd, force, counts):
    return pl.pallas_call(
        far_kernel,
        out_shape=[f32(*FORCE_SHAPE), f32(*COUNT_SHAPE), f32(*GRAD_SHAPE), f32(devices, 2, POINTS)],
        in_specs=[VMEM, SMEM] + [VMEM] * 4,
        out_specs=[VMEM] * 4,
        scratch_shapes=ghost_space(6),
        input_output_aliases={4: 0, 5: 1},
        compiler_params=PARAMS,
        cost_estimate=cost(12),
        name="far",
    )(target, table, from_even, from_odd, force, counts)[2:]


def body(positions, cell_points, target_log, export_count, export_cell, import_pair, import_shift):
    devices = export_count.shape[1]
    inputs = (
        positions, cell_points, target_log, export_count,
        jnp.transpose(export_cell, (2, 0, 1)),
        jnp.transpose(import_pair, (2, 0, 1)),
        jnp.transpose(import_shift, (0, 3, 1, 2)),
    )
    target, logs, table, *messages = pl.pallas_call(
        first_kernel,
        out_shape=[f32(*CELL_SHAPE), f32(BINS, POINTS), jax.ShapeDtypeStruct((TABLE,), jnp.int32)] + MESSAGES,
        in_specs=[pl.BlockSpec(memory_space=pltpu.HBM)] * 7,
        out_specs=[VMEM, VMEM, SMEM] + [VMEM] * 4,
        scratch_shapes=[
            pltpu.VMEM(positions.shape, jnp.float32),
            pltpu.SMEM(cell_points.shape, jnp.int32),
            pltpu.SMEM(target_log.shape, jnp.float32),
            pltpu.SMEM(export_count.shape, jnp.int32),
            pltpu.SMEM((SLOTS, 1, devices), jnp.int32),
            pltpu.SMEM((SLOTS, 1, devices), jnp.int32),
            pltpu.SMEM((3, SLOTS, 1, devices), jnp.int32),
            pltpu.VMEM(CELL_SHAPE, jnp.float32),
            pltpu.SemaphoreType.DMA((7,)),
        ],
        compiler_params=PARAMS,
        name="first",
    )(*(pltpu.with_memory_space_constraint(value, pltpu.HBM) for value in inputs))
    for iteration in range(STEPS):
        depth_even, depth_odd, sky_even, sky_odd = messages
        depth_even, depth_odd = swap(depth_even, "depth", 1), swap(depth_odd, "depth", 2)
        depth_even, depth_odd, force, counts = lax.optimization_barrier(
            (depth_even, depth_odd, *self_pairs(target, table))
        )
        near = near_pairs(target, table, depth_even, depth_odd, force, counts)
        sky_even = swap(jnp.stack([sky_even, depth_even[1], depth_odd[1]]), "sky", 1)
        sky_odd = swap(jnp.stack([sky_odd, depth_even[2], depth_odd[2]]), "sky", 2)
        grad, payload = far_pairs(devices, target, table, sky_even, sky_odd, *near)
        sums = lax.all_to_all(payload, AXES, 0, 0)
        if iteration == STEPS - 1:
            return pl.pallas_call(
                last_kernel,
                out_shape=f32(*positions.shape),
                in_specs=[VMEM] * 4,
                out_specs=VMEM,
                compiler_params=PARAMS,
                name="last",
            )(sums, grad, travel, logs)
        travel, target, *messages = pl.pallas_call(
            update_kernel,
            out_shape=[f32(*CELL_SHAPE), f32(*CELL_SHAPE)] + MESSAGES,
            in_specs=[VMEM] * 4 + [SMEM],
            out_specs=[VMEM] * 6,
            scratch_shapes=[pltpu.VMEM(CELL_SHAPE, jnp.float32)],
            compiler_params=PARAMS,
            name="update",
        )(sums, grad, target, logs, table)


def solution(mesh):
    in_specs = (
        P(None, ("sky", "depth"), None),
        P(("sky", "depth")),
        P(),
        P(("sky", "depth"), None),
        P(("sky", "depth"), None, None),
        P(("sky", "depth"), None, None),
        P(None, ("sky", "depth"), None, None),
    )
    out_specs = P(None, ("sky", "depth"), None)
    return jax.shard_map(body, mesh=mesh, in_specs=in_specs, out_specs=out_specs, check_vma=False)
```

profile of v0, /device:TPU:1, one launch (start us, length us, event | category | flops | bytes accessed | tf_op | source)
XLA Modules:
  0.0 91.5 jit_solution(2656396709847499983)
XLA Ops:
  0.0 1.9 %first.1 = (f32[16,4,128]{2,1,0:T(4,128)S(1)}, f32[16,128]{1,0:T(8,128)S(1)}, s32[144]{0:T(256)S(1)}, f32[3,7,4,128]{3,2,1,0:T(4,128)S(1)}, f32[3,7,4,128]{3,2,1...) custom-call(f32[3,16,128]{2,1,0:T(8,128)} %positions_in.1, s32[16]{0:T(128)} %points_in.1, ...), custom_call_target="tpu_custom_call" | custom-call | tf_op jit(solution)/shard_map/first/pallas_call | solution.py:476
  1.9 1.5 %collective-permute-start = (f32[3,7,4,128]{3,2,1,0:T(4,128)S(1)}, f32[3,7,4,128]{3,2,1,0:T(4,128)S(1)}, u32[]{:S(2)}, u32[]{:S(2)}) collective-permute-start(f32[3,7,4,128]{3,2,1,0:T(4,128)S(1)} %get-tuple-element.41), channel_id=1, source_target_pairs={{0,1},{1,0},{2,3},{3,2},{4,5},{5,4},{6,7},{7,6},{8,9},{9,8},{10,11... | collective-permute-start | bytes 129032 | tf_op jit(solution)/shard_map/ppermute | solution.py:402
  3.4 3.2 %collective-permute-start.1 = (f32[3,7,4,128]{3,2,1,0:T(4,128)S(1)}, f32[3,7,4,128]{3,2,1,0:T(4,128)S(1)}, u32[]{:S(2)}, u32[]{:S(2)}) collective-permute-start(f32[3,7,4,128]{3,2,1,0:T(4,128)S(1)} %get-tuple-element.42), channel_id=1, source_target_pairs={{1,2},{2,1},{3,4},{4,3},{5,6},{6,5},{9,10},{10,9},{11,12},{12,11},... | collective-permute-start | bytes 129032 | tf_op jit(solution)/shard_map/ppermute | solution.py:402
  6.6 5.9 %self.2 = (f32[16,48,8,128]{3,2,1,0:T(8,128)S(1)}, f32[16,8,128]{2,1,0:T(8,128)S(1)}) custom-call(f32[16,4,128]{2,1,0:T(4,128)S(1)} %get-tuple-element.38.target, s32[144]{0:T(256)S(1)} %get-tuple-element.39.table), custom_call_target="tpu_custom_call" | custom-call | bytes 18000000 | tf_op jit(solution)/shard_map/self/pallas_call | solution.py:427
  12.6 0.0 collective-permute-done.from_even
  12.6 0.0 collective-permute-done.1.from_odd
  12.6 0.8 collective-permute-start.2
  13.4 4.6 %collective-permute-start.3 = (f32[3,7,4,128]{3,2,1,0:T(4,128)S(1)}, f32[3,7,4,128]{3,2,1,0:T(4,128)S(1)}, u32[]{:S(2)}, u32[]{:S(2)}) collective-permute-start(f32[3,7,4,128]{3,2,1,0:T(4,128)S(1)} %pad_maximum_fusion.1), channel_id=1, source_target_pairs={{8,16},{16,8},{24,32},{32,24},{40,48},{48,40},{56,64},{64,56},{72,... | collective-permute-start | bytes 129032 | tf_op jit(solution)/shard_map/ppermute | solution.py:402
  18.1 3.3 %near.2 = (f32[16,48,8,128]{3,2,1,0:T(8,128)S(1)}, f32[16,8,128]{2,1,0:T(8,128)S(1)}) custom-call(f32[16,4,128]{2,1,0:T(4,128)S(1)} %get-tuple-element.38.target, s32[144]{0:T(256)S(1)} %get-tuple-element.39.table, f32[3,7,4,128]{3,2,1,0:T(4,128)S(1)} %collective-permute-done.from_even, ...), custom_call_target="tpu_custom_call", output_to_operand_aliasing={{0}: (4, {}), {1}: (5, {})} | custom-call | bytes 12000000 | tf_op jit(solution)/shard_map/near/pallas_call | solution.py:441
  21.4 0.0 collective-permute-done.2.from_even
  21.4 0.0 collective-permute-done.3.from_odd
  21.4 7.8 %far.2 = (f32[16,48,8,128]{3,2,1,0:T(8,128)S(1)}, f32[16,8,128]{2,1,0:T(8,128)S(1)}, f32[16,6144]{1,0:T(8,128)S(1)}, f32[128,2,128]{2,1,0:T(2,128)S(1)}) custom-call(f32[16,4,128]{2,1,0:T(4,128)S(1)} %get-tuple-element.38.target, s32[144]{0:T(256)S(1)} %get-tuple-element.39.table, ...), custom_call_target="tpu_custom_call", output_to_operand_aliasing={{0}: (4, {}), {1}: (5, {})} | custom-call | bytes 36000000 | tf_op jit(solution)/shard_map/far/pallas_call | solution.py:455
  29.2 19.0 %all_to_all.10.sums = f32[128,2,128]{2,1,0:T(2,128)S(1)} all-to-all(f32[128,2,128]{2,1,0:T(2,128)S(1)} %get-tuple-element.52), channel_id=1, replica_groups=mesh['sky'=16,'depth'=8] {'sky','depth'}, dimensions={0} | all-to-all | bytes 262144 | tf_op jit(solution)/shard_map/all_to_all | solution.py:505
  48.2 1.1 %update.1 = (f32[16,4,128]{2,1,0:T(4,128)S(1)}, f32[16,4,128]{2,1,0:T(4,128)S(1)}, f32[3,7,4,128]{3,2,1,0:T(4,128)S(1)}, f32[3,7,4,128]{3,2,1,0:T(4,128)S(1)}, f...) custom-call(f32[128,2,128]{2,1,0:T(2,128)S(1)} %all_to_all.10.sums, f32[16,6144]{1,0:T(8,128)S(1)} %get-tuple-element.53.grad, ...), custom_call_target="tpu_custom_call" | custom-call | tf_op jit(solution)/shard_map/update/pallas_call | solution.py:515
  49.3 0.8 collective-permute-start.4
  50.1 2.1 %collective-permute-start.5 = (f32[3,7,4,128]{3,2,1,0:T(4,128)S(1)}, f32[3,7,4,128]{3,2,1,0:T(4,128)S(1)}, u32[]{:S(2)}, u32[]{:S(2)}) collective-permute-start(f32[3,7,4,128]{3,2,1,0:T(4,128)S(1)} %get-tuple-element.58), channel_id=1, source_target_pairs={{1,2},{2,1},{3,4},{4,3},{5,6},{6,5},{9,10},{10,9},{11,12},{12,11},... | collective-permute-start | bytes 129032 | tf_op jit(solution)/shard_map/ppermute | solution.py:402
  52.2 5.9 %self.3 = (f32[16,48,8,128]{3,2,1,0:T(8,128)S(1)}, f32[16,8,128]{2,1,0:T(8,128)S(1)}) custom-call(f32[16,4,128]{2,1,0:T(4,128)S(1)} %get-tuple-element.55.target, s32[144]{0:T(256)S(1)} %get-tuple-element.39.table), custom_call_target="tpu_custom_call" | custom-call | bytes 18000000 | tf_op jit(solution)/shard_map/self/pallas_call | solution.py:427
  58.1 0.0 collective-permute-done.4.from_even
  58.1 0.0 collective-permute-done.5.from_odd
  58.2 0.1 collective-permute-start.6
  58.3 1.2 %collective-permute-start.7 = (f32[3,7,4,128]{3,2,1,0:T(4,128)S(1)}, f32[3,7,4,128]{3,2,1,0:T(4,128)S(1)}, u32[]{:S(2)}, u32[]{:S(2)}) collective-permute-start(f32[3,7,4,128]{3,2,1,0:T(4,128)S(1)} %pad_maximum_fusion.3), channel_id=1, source_target_pairs={{8,16},{16,8},{24,32},{32,24},{40,48},{48,40},{56,64},{64,56},{72,... | collective-permute-start | bytes 129032 | tf_op jit(solution)/shard_map/ppermute | solution.py:402
  59.6 3.3 %near.3 = (f32[16,48,8,128]{3,2,1,0:T(8,128)S(1)}, f32[16,8,128]{2,1,0:T(8,128)S(1)}) custom-call(f32[16,4,128]{2,1,0:T(4,128)S(1)} %get-tuple-element.55.target, s32[144]{0:T(256)S(1)} %get-tuple-element.39.table, f32[3,7,4,128]{3,2,1,0:T(4,128)S(1)} %collective-permute-done.4.from_even, ...), custom_call_target="tpu_custom_call", output_to_operand_aliasing={{0}: (4, {}), {1}: (5, {})} | custom-call | bytes 12000000 | tf_op jit(solution)/shard_map/near/pallas_call | solution.py:441
  62.9 0.0 collective-permute-done.6.from_even
  62.9 2.4 %collective-permute-done.7.from_odd = f32[3,7,4,128]{3,2,1,0:T(4,128)S(1)} collective-permute-done((f32[3,7,4,128]{3,2,1,0:T(4,128)S(1)}, f32[3,7,4,128]{3,2,1,0:T(4,128)S(1)}, u32[]{:S(2)}, u32[]{:S(2)}) %collective-permute-start.7) | collective-permute-done | bytes 43040 | tf_op jit(solution)/shard_map/ppermute | solution.py:402
  65.3 7.8 %far.3 = (f32[16,48,8,128]{3,2,1,0:T(8,128)S(1)}, f32[16,8,128]{2,1,0:T(8,128)S(1)}, f32[16,6144]{1,0:T(8,128)S(1)}, f32[128,2,128]{2,1,0:T(2,128)S(1)}) custom-call(f32[16,4,128]{2,1,0:T(4,128)S(1)} %get-tuple-element.55.target, s32[144]{0:T(256)S(1)} %get-tuple-element.39.table, ...), custom_call_target="tpu_custom_call", output_to_operand_aliasing={{0}: (4, {}), {1}: (5, {})} | custom-call | bytes 36000000 | tf_op jit(solution)/shard_map/far/pallas_call | solution.py:455
  73.0 17.5 %all_to_all.11.sums = f32[128,2,128]{2,1,0:T(2,128)S(1)} all-to-all(f32[128,2,128]{2,1,0:T(2,128)S(1)} %get-tuple-element.68), channel_id=1, replica_groups=mesh['sky'=16,'depth'=8] {'sky','depth'}, dimensions={0} | all-to-all | bytes 262144 | tf_op jit(solution)/shard_map/all_to_all | solution.py:505
  90.5 1.0 %last.1 = f32[3,16,128]{2,1,0:T(8,128)} custom-call(f32[128,2,128]{2,1,0:T(2,128)S(1)} %all_to_all.11.sums, f32[16,6144]{1,0:T(8,128)S(1)} %get-tuple-element.69.grad, f32[16,4,128]{2,1,0:T(4,128)S(1)} %get-tuple-element.70.travel, f32[16,128]{1,0:T(8,128)S(1)} %get-tuple-element.54.logs), custom_call_target="tpu_custom_call" | custom-call | tf_op jit(solution)/shard_map/last/pallas_call | solution.py:507
  (7 shorter events, 0.1 us)
Async XLA Ops:
  1.9 10.6 %collective-permute-start = (f32[3,7,4,128]{3,2,1,0:T(4,128)S(1)}, f32[3,7,4,128]{3,2,1,0:T(4,128)S(1)}, u32[]{:S(2)}, u32[]{:S(2)}) collective-permute-start(f32[3,7,4,128]{3,2,1,0:T(4,128)S(1)} %get-tuple-element.41), channel_id=1, source_target_pairs={{0,1},{1,0},{2,3},{3,2},{4,5},{5,4},{6,7},{7,6},{8,9},{9,8},{10,11... | collective-permute-start | bytes 129032 | tf_op jit(solution)/shard_map/ppermute | solution.py:402
  3.4 9.1 %collective-permute-start.1 = (f32[3,7,4,128]{3,2,1,0:T(4,128)S(1)}, f32[3,7,4,128]{3,2,1,0:T(4,128)S(1)}, u32[]{:S(2)}, u32[]{:S(2)}) collective-permute-start(f32[3,7,4,128]{3,2,1,0:T(4,128)S(1)} %get-tuple-element.42), channel_id=1, source_target_pairs={{1,2},{2,1},{3,4},{4,3},{5,6},{6,5},{9,10},{10,9},{11,12},{12,11},... | collective-permute-start | bytes 129032 | tf_op jit(solution)/shard_map/ppermute | solution.py:402
  12.6 8.8 %collective-permute-start.2 = (f32[3,7,4,128]{3,2,1,0:T(4,128)S(1)}, f32[3,7,4,128]{3,2,1,0:T(4,128)S(1)}, u32[]{:S(2)}, u32[]{:S(2)}) collective-permute-start(f32[3,7,4,128]{3,2,1,0:T(4,128)S(1)} %pad_maximum_fusion), channel_id=1, source_target_pairs={{0,8},{8,0},{16,24},{24,16},{32,40},{40,32},{48,56},{56,48},{64,72... | collective-permute-start | bytes 129032 | tf_op jit(solution)/shard_map/ppermute | solution.py:402
  13.4 8.0 %collective-permute-start.3 = (f32[3,7,4,128]{3,2,1,0:T(4,128)S(1)}, f32[3,7,4,128]{3,2,1,0:T(4,128)S(1)}, u32[]{:S(2)}, u32[]{:S(2)}) collective-permute-start(f32[3,7,4,128]{3,2,1,0:T(4,128)S(1)} %pad_maximum_fusion.1), channel_id=1, source_target_pairs={{8,16},{16,8},{24,32},{32,24},{40,48},{48,40},{56,64},{64,56},{72,... | collective-permute-start | bytes 129032 | tf_op jit(solution)/shard_map/ppermute | solution.py:402
  49.3 8.8 %collective-permute-start.4 = (f32[3,7,4,128]{3,2,1,0:T(4,128)S(1)}, f32[3,7,4,128]{3,2,1,0:T(4,128)S(1)}, u32[]{:S(2)}, u32[]{:S(2)}) collective-permute-start(f32[3,7,4,128]{3,2,1,0:T(4,128)S(1)} %get-tuple-element.57), channel_id=1, source_target_pairs={{0,1},{1,0},{2,3},{3,2},{4,5},{5,4},{6,7},{7,6},{8,9},{9,8},{10,11... | collective-permute-start | bytes 129032 | tf_op jit(solution)/shard_map/ppermute | solution.py:402
  50.1 8.1 %collective-permute-start.5 = (f32[3,7,4,128]{3,2,1,0:T(4,128)S(1)}, f32[3,7,4,128]{3,2,1,0:T(4,128)S(1)}, u32[]{:S(2)}, u32[]{:S(2)}) collective-permute-start(f32[3,7,4,128]{3,2,1,0:T(4,128)S(1)} %get-tuple-element.58), channel_id=1, source_target_pairs={{1,2},{2,1},{3,4},{4,3},{5,6},{6,5},{9,10},{10,9},{11,12},{12,11},... | collective-permute-start | bytes 129032 | tf_op jit(solution)/shard_map/ppermute | solution.py:402
  58.2 4.7 %collective-permute-start.6 = (f32[3,7,4,128]{3,2,1,0:T(4,128)S(1)}, f32[3,7,4,128]{3,2,1,0:T(4,128)S(1)}, u32[]{:S(2)}, u32[]{:S(2)}) collective-permute-start(f32[3,7,4,128]{3,2,1,0:T(4,128)S(1)} %pad_maximum_fusion.2), channel_id=1, source_target_pairs={{0,8},{8,0},{16,24},{24,16},{32,40},{40,32},{48,56},{56,48},{64,72... | collective-permute-start | bytes 129032 | tf_op jit(solution)/shard_map/ppermute | solution.py:402
  58.3 7.0 %collective-permute-start.7 = (f32[3,7,4,128]{3,2,1,0:T(4,128)S(1)}, f32[3,7,4,128]{3,2,1,0:T(4,128)S(1)}, u32[]{:S(2)}, u32[]{:S(2)}) collective-permute-start(f32[3,7,4,128]{3,2,1,0:T(4,128)S(1)} %pad_maximum_fusion.3), channel_id=1, source_target_pairs={{8,16},{16,8},{24,32},{32,24},{40,48},{48,40},{56,64},{64,56},{72,... | collective-permute-start | bytes 129032 | tf_op jit(solution)/shard_map/ppermute | solution.py:402
where the time goes:
time: 92.2 us; the launch traced here: 91.5 us
  Pallas kernels  38.1 us (41%)
  blocking collectives  36.4 us (39%)
  starting transfers between devices  14.3 us (16%)
  waiting for transfers between devices  2.39 us (3%)
    all_to_all x2, blocking collectives, body(): sums = lax.all_to_all(payload, AXES, 0, 0)  36.4 us
    pallas_call x2, Pallas kernels, far_pairs(): pl.pallas_call(far_kernel, out_shape=[f32(*FORCE_SHAPE), f32(*COUNT_SHAPE...  15.5 us
    ppermute x8, starting transfers between devices, swap(): return lax.ppermute(value, axis, perm)  14.3 us
    pallas_call x2, Pallas kernels, self_pairs(): pl.pallas_call(self_kernel, out_shape=[f32(*FORCE_SHAPE), f32(*COUNT_SHAP...  11.9 us
    pallas_call x2, Pallas kernels, near_pairs(): pl.pallas_call(near_kernel, out_shape=[f32(*FORCE_SHAPE), f32(*COUNT_SHAP...  6.65 us
    ppermute x8, waiting for transfers between devices, swap(): return lax.ppermute(value, axis, perm)  2.39 us
    pallas_call x1, Pallas kernels, body(): pl.pallas_call(first_kernel, out_shape=[f32(*CELL_SHAPE), f32(BINS, POINT...  1.92 us
  transfers between devices with their start and end apart: 8, of which 1 were waited for; matrix products, arithmetic and copies ran while one was open for 0% of the time, Pallas kernels for 20%

commit v1 on v0

--- a/solution.py
+++ b/solution.py
@@ -31,7 +31,7 @@
 ]
 FORCE_SCALE = [-256.0 / UNIT * scale for scale in COUNT_SCALE]
 
-NEIGHBOURS = [(0, 1), (0, 2), (1, 0), (1, 1), (1, 2), (2, 0), (2, 1), (2, 2)]
+NEIGHBOURS = [(1, 0), (2, 0), (0, 1), (1, 1), (2, 1), (0, 2), (1, 2), (2, 2)]
 TABLE_ROW = 16
 EXPORT, IMPORT, LIVE, SHIFT = 0, SLOTS, 2 * SLOTS, 2 * SLOTS + 1
 SIZES = len(NEIGHBOURS) * TABLE_ROW
@@ -79,13 +79,13 @@
 
 
 def pack(source, table, outs):
-    depth_even, depth_odd, sky_even, sky_odd = outs
+    sky_even, sky_odd, depth_even, depth_odd = outs
     lanes = lax.broadcasted_iota(jnp.int32, (4, POINTS), 1)
     for index, (sky_option, depth_option) in enumerate(NEIGHBOURS):
-        if depth_option == 0:
-            out = sky_even if sky_option == 1 else sky_odd
+        if sky_option == 0:
+            out = depth_even if depth_option == 1 else depth_odd
         else:
-            out = (depth_even if depth_option == 1 else depth_odd).at[sky_option]
+            out = (sky_even if sky_option == 1 else sky_odd).at[depth_option]
         row = index * TABLE_ROW
         live = table[row + LIVE]
         meta = jnp.zeros((4, POINTS), jnp.float32)
@@ -103,7 +103,7 @@
 
 def first_kernel(
     positions_in, points_in, logs_in, count_in, export_in, import_in, shift_in,
-    target, logs, table, depth_even, depth_odd, sky_even, sky_odd,
+    target, logs, table, sky_even, sky_odd, depth_even, depth_odd,
     positions, points, log_list, count, exports, imports, shifts, source, sems,
 ):
     pairs = [
@@ -137,7 +137,7 @@
         live = lanes < points[cell]
         target[cell] = jnp.where(live, tile, -FAR)
         source[cell] = jnp.where(live, tile, FAR)
-    pack(source, table, (depth_even, depth_odd, sky_even, sky_odd))
+    pack(source, table, (sky_even, sky_odd, depth_even, depth_odd))
 
 
 def shape_pairs(at, row_list, cell_list, source, base, target):
@@ -362,7 +362,7 @@
 
 def update_kernel(
     sums, grad, target, logs, table,
-    travel, next_target, depth_even, depth_odd, sky_even, sky_odd, source,
+    travel, next_target, sky_even, sky_odd, depth_even, depth_odd, source,
 ):
     lanes = lax.broadcasted_iota(jnp.int32, (4, POINTS), 1)
     moves = moves_of(sums, grad, logs)
@@ -372,7 +372,7 @@
         tile = target[cell] + (STEP_SIZE * UNIT) * tile
         next_target[cell] = tile
         source[cell] = jnp.where(lanes < table[SIZES + cell], tile, FAR)
-    pack(source, table, (depth_even, depth_odd, sky_even, sky_odd))
+    pack(source, table, (sky_even, sky_odd, depth_even, depth_odd))
 
 
 def last_kernel(sums, grad, travel, logs, out):
@@ -493,15 +493,15 @@
         name="first",
     )(*(pltpu.with_memory_space_constraint(value, pltpu.HBM) for value in inputs))
     for iteration in range(STEPS):
-        depth_even, depth_odd, sky_even, sky_odd = messages
-        depth_even, depth_odd = swap(depth_even, "depth", 1), swap(depth_odd, "depth", 2)
-        depth_even, depth_odd, force, counts = lax.optimization_barrier(
-            (depth_even, depth_odd, *self_pairs(target, table))
+        sky_even, sky_odd, depth_even, depth_odd = messages
+        sky_even, sky_odd = swap(sky_even, "sky", 1), swap(sky_odd, "sky", 2)
+        sky_even, sky_odd, force, counts = lax.optimization_barrier(
+            (sky_even, sky_odd, *self_pairs(target, table))
         )
-        near = near_pairs(target, table, depth_even, depth_odd, force, counts)
-        sky_even = swap(jnp.stack([sky_even, depth_even[1], depth_odd[1]]), "sky", 1)
-        sky_odd = swap(jnp.stack([sky_odd, depth_even[2], depth_odd[2]]), "sky", 2)
-        grad, payload = far_pairs(devices, target, table, sky_even, sky_odd, *near)
+        near = near_pairs(target, table, sky_even, sky_odd, force, counts)
+        depth_even = swap(jnp.stack([depth_even, sky_even[1], sky_odd[1]]), "depth", 1)
+        depth_odd = swap(jnp.stack([depth_odd, sky_even[2], sky_odd[2]]), "depth", 2)
+        grad, payload = far_pairs(devices, target, table, depth_even, depth_odd, *near)
         sums = lax.all_to_all(payload, AXES, 0, 0)
         if iteration == STEPS - 1:
             return pl.pallas_call(

time: 92.2 us -> 89.9 us (0.975)
  starting transfers between devices: 14.3 us -> 19.2 us
  Pallas kernels: 38.1 us -> 33.5 us
  waiting for transfers between devices: 2.39 us -> 0.53 us
  blocking collectives: 36.4 us -> 34.8 us
    ppermute x8, starting transfers between devices: 14.3 us -> 19.2 us  [swap(): return lax.ppermute(value, axis, perm)]
    ppermute x8, waiting for transfers between devices: 2.39 us -> 0.53 us  [swap(): return lax.ppermute(value, axis, perm)]
    pallas_call x2, Pallas kernels: 11.9 us -> 10 us  [self_pairs(): pl.pallas_call(self_kernel, out_shape=[f32(*FORCE_SHAPE), f32(*COUNT_SHAP...]
    pallas_call x2, Pallas kernels: 6.65 us -> 4.82 us  [near_pairs(): pl.pallas_call(near_kernel, out_shape=[f32(*FORCE_SHAPE), f32(*COUNT_SHAP...]
    all_to_all x2, blocking collectives: 36.4 us -> 34.8 us  [body(): sums = lax.all_to_all(payload, AXES, 0, 0)]
    pallas_call x2, Pallas kernels: 15.5 us -> 14.5 us  [far_pairs(): pl.pallas_call(far_kernel, out_shape=[f32(*FORCE_SHAPE), f32(*COUNT_SHAPE...]
  transfers between devices with their start and end apart: 8 -> 8, of which waited for: 1 -> 1; matrix products, arithmetic and copies ran while one was open for 0% -> 0% of each run, Pallas kernels for 20% -> 17%
where the time goes in v1:
time: 89.9 us; the launch traced here: 88.3 us
  blocking collectives  34.8 us (39%)
  Pallas kernels  33.5 us (37%)
  starting transfers between devices  19.2 us (21%)
    all_to_all x2, blocking collectives, body(): sums = lax.all_to_all(payload, AXES, 0, 0)  34.8 us
    ppermute x8, starting transfers between devices, swap(): return lax.ppermute(value, axis, perm)  19.2 us
    pallas_call x2, Pallas kernels, far_pairs(): pl.pallas_call(far_kernel, out_shape=[f32(*FORCE_SHAPE), f32(*COUNT_SHAPE...  14.5 us
    pallas_call x2, Pallas kernels, self_pairs(): pl.pallas_call(self_kernel, out_shape=[f32(*FORCE_SHAPE), f32(*COUNT_SHAP...  10 us
    pallas_call x2, Pallas kernels, near_pairs(): pl.pallas_call(near_kernel, out_shape=[f32(*FORCE_SHAPE), f32(*COUNT_SHAP...  4.82 us
    pallas_call x1, Pallas kernels, body(): pl.pallas_call(first_kernel, out_shape=[f32(*CELL_SHAPE), f32(BINS, POINT...  1.92 us
  transfers between devices with their start and end apart: 8, of which 1 were waited for; matrix products, arithmetic and copies ran while one was open for 0% of the time, Pallas kernels for 17%

profile of v1, /device:TPU:1, one launch (start us, length us, event | category | flops | bytes accessed | tf_op | source)
XLA Modules:
  0.0 88.3 jit_solution(16978128869811236628)
XLA Ops:
  0.0 1.9 %first.1 = (f32[16,4,128]{2,1,0:T(4,128)S(1)}, f32[16,128]{1,0:T(8,128)S(1)}, s32[144]{0:T(256)S(1)}, f32[3,7,4,128]{3,2,1,0:T(4,128)S(1)}, f32[3,7,4,128]{3,2,1...) custom-call(f32[3,16,128]{2,1,0:T(8,128)} %positions_in.1, s32[16]{0:T(128)} %points_in.1, ...), custom_call_target="tpu_custom_call" | custom-call | tf_op jit(solution)/shard_map/first/pallas_call | solution.py:476
  1.9 2.5 %collective-permute-start = (f32[3,7,4,128]{3,2,1,0:T(4,128)S(1)}, f32[3,7,4,128]{3,2,1,0:T(4,128)S(1)}, u32[]{:S(2)}, u32[]{:S(2)}) collective-permute-start(f32[3,7,4,128]{3,2,1,0:T(4,128)S(1)} %get-tuple-element.41), channel_id=1, source_target_pairs={{0,8},{8,0},{16,24},{24,16},{32,40},{40,32},{48,56},{56,48},{64,72... | collective-permute-start | bytes 129032 | tf_op jit(solution)/shard_map/ppermute | solution.py:402
  4.5 4.4 %collective-permute-start.1 = (f32[3,7,4,128]{3,2,1,0:T(4,128)S(1)}, f32[3,7,4,128]{3,2,1,0:T(4,128)S(1)}, u32[]{:S(2)}, u32[]{:S(2)}) collective-permute-start(f32[3,7,4,128]{3,2,1,0:T(4,128)S(1)} %get-tuple-element.42), channel_id=1, source_target_pairs={{8,16},{16,8},{24,32},{32,24},{40,48},{48,40},{56,64},{64,56},{72,... | collective-permute-start | bytes 129032 | tf_op jit(solution)/shard_map/ppermute | solution.py:402
  8.9 5.0 %self.2 = (f32[16,48,8,128]{3,2,1,0:T(8,128)S(1)}, f32[16,8,128]{2,1,0:T(8,128)S(1)}) custom-call(f32[16,4,128]{2,1,0:T(4,128)S(1)} %get-tuple-element.38.target, s32[144]{0:T(256)S(1)} %get-tuple-element.39.table), custom_call_target="tpu_custom_call" | custom-call | bytes 18000000 | tf_op jit(solution)/shard_map/self/pallas_call | solution.py:427
  13.9 0.0 collective-permute-done.from_even
  13.9 0.0 collective-permute-done.1.from_odd
  14.0 2.2 %collective-permute-start.2 = (f32[3,7,4,128]{3,2,1,0:T(4,128)S(1)}, f32[3,7,4,128]{3,2,1,0:T(4,128)S(1)}, u32[]{:S(2)}, u32[]{:S(2)}) collective-permute-start(f32[3,7,4,128]{3,2,1,0:T(4,128)S(1)} %pad_maximum_fusion), channel_id=1, source_target_pairs={{0,1},{1,0},{2,3},{3,2},{4,5},{5,4},{6,7},{7,6},{8,9},{9,8},{10,11... | collective-permute-start | bytes 129032 | tf_op jit(solution)/shard_map/ppermute | solution.py:402
  16.2 3.3 %collective-permute-start.3 = (f32[3,7,4,128]{3,2,1,0:T(4,128)S(1)}, f32[3,7,4,128]{3,2,1,0:T(4,128)S(1)}, u32[]{:S(2)}, u32[]{:S(2)}) collective-permute-start(f32[3,7,4,128]{3,2,1,0:T(4,128)S(1)} %pad_maximum_fusion.1), channel_id=1, source_target_pairs={{1,2},{2,1},{3,4},{4,3},{5,6},{6,5},{9,10},{10,9},{11,12},{12,11},... | collective-permute-start | bytes 129032 | tf_op jit(solution)/shard_map/ppermute | solution.py:402
  19.6 2.4 %near.2 = (f32[16,48,8,128]{3,2,1,0:T(8,128)S(1)}, f32[16,8,128]{2,1,0:T(8,128)S(1)}) custom-call(f32[16,4,128]{2,1,0:T(4,128)S(1)} %get-tuple-element.38.target, s32[144]{0:T(256)S(1)} %get-tuple-element.39.table, f32[3,7,4,128]{3,2,1,0:T(4,128)S(1)} %collective-permute-done.from_even, ...), custom_call_target="tpu_custom_call", output_to_operand_aliasing={{0}: (4, {}), {1}: (5, {})} | custom-call | bytes 12000000 | tf_op jit(solution)/shard_map/near/pallas_call | solution.py:441
  22.0 0.0 collective-permute-done.2.from_even
  22.0 0.0 collective-permute-done.3.from_odd
  22.0 7.3 %far.2 = (f32[16,48,8,128]{3,2,1,0:T(8,128)S(1)}, f32[16,8,128]{2,1,0:T(8,128)S(1)}, f32[16,6144]{1,0:T(8,128)S(1)}, f32[128,2,128]{2,1,0:T(2,128)S(1)}) custom-call(f32[16,4,128]{2,1,0:T(4,128)S(1)} %get-tuple-element.38.target, s32[144]{0:T(256)S(1)} %get-tuple-element.39.table, ...), custom_call_target="tpu_custom_call", output_to_operand_aliasing={{0}: (4, {}), {1}: (5, {})} | custom-call | bytes 36000000 | tf_op jit(solution)/shard_map/far/pallas_call | solution.py:455
  29.3 17.2 %all_to_all.10.sums = f32[128,2,128]{2,1,0:T(2,128)S(1)} all-to-all(f32[128,2,128]{2,1,0:T(2,128)S(1)} %get-tuple-element.52), channel_id=1, replica_groups=mesh['sky'=16,'depth'=8] {'sky','depth'}, dimensions={0} | all-to-all | bytes 262144 | tf_op jit(solution)/shard_map/all_to_all | solution.py:505
  46.5 1.1 %update.1 = (f32[16,4,128]{2,1,0:T(4,128)S(1)}, f32[16,4,128]{2,1,0:T(4,128)S(1)}, f32[3,7,4,128]{3,2,1,0:T(4,128)S(1)}, f32[3,7,4,128]{3,2,1,0:T(4,128)S(1)}, f...) custom-call(f32[128,2,128]{2,1,0:T(2,128)S(1)} %all_to_all.10.sums, f32[16,6144]{1,0:T(8,128)S(1)} %get-tuple-element.53.grad, ...), custom_call_target="tpu_custom_call" | custom-call | tf_op jit(solution)/shard_map/update/pallas_call | solution.py:515
  47.7 0.4 collective-permute-start.4
  48.1 2.0 %collective-permute-start.5 = (f32[3,7,4,128]{3,2,1,0:T(4,128)S(1)}, f32[3,7,4,128]{3,2,1,0:T(4,128)S(1)}, u32[]{:S(2)}, u32[]{:S(2)}) collective-permute-start(f32[3,7,4,128]{3,2,1,0:T(4,128)S(1)} %get-tuple-element.58), channel_id=1, source_target_pairs={{8,16},{16,8},{24,32},{32,24},{40,48},{48,40},{56,64},{64,56},{72,... | collective-permute-start | bytes 129032 | tf_op jit(solution)/shard_map/ppermute | solution.py:402
  50.0 5.0 %self.3 = (f32[16,48,8,128]{3,2,1,0:T(8,128)S(1)}, f32[16,8,128]{2,1,0:T(8,128)S(1)}) custom-call(f32[16,4,128]{2,1,0:T(4,128)S(1)} %get-tuple-element.55.target, s32[144]{0:T(256)S(1)} %get-tuple-element.39.table), custom_call_target="tpu_custom_call" | custom-call | bytes 18000000 | tf_op jit(solution)/shard_map/self/pallas_call | solution.py:427
  55.0 0.0 collective-permute-done.4.from_even
  55.1 0.0 collective-permute-done.5.from_odd
  55.1 1.9 %collective-permute-start.6 = (f32[3,7,4,128]{3,2,1,0:T(4,128)S(1)}, f32[3,7,4,128]{3,2,1,0:T(4,128)S(1)}, u32[]{:S(2)}, u32[]{:S(2)}) collective-permute-start(f32[3,7,4,128]{3,2,1,0:T(4,128)S(1)} %pad_maximum_fusion.2), channel_id=1, source_target_pairs={{0,1},{1,0},{2,3},{3,2},{4,5},{5,4},{6,7},{7,6},{8,9},{9,8},{10,11... | collective-permute-start | bytes 129032 | tf_op jit(solution)/shard_map/ppermute | solution.py:402
  57.1 2.4 %collective-permute-start.7 = (f32[3,7,4,128]{3,2,1,0:T(4,128)S(1)}, f32[3,7,4,128]{3,2,1,0:T(4,128)S(1)}, u32[]{:S(2)}, u32[]{:S(2)}) collective-permute-start(f32[3,7,4,128]{3,2,1,0:T(4,128)S(1)} %pad_maximum_fusion.3), channel_id=1, source_target_pairs={{1,2},{2,1},{3,4},{4,3},{5,6},{6,5},{9,10},{10,9},{11,12},{12,11},... | collective-permute-start | bytes 129032 | tf_op jit(solution)/shard_map/ppermute | solution.py:402
  59.5 2.4 %near.3 = (f32[16,48,8,128]{3,2,1,0:T(8,128)S(1)}, f32[16,8,128]{2,1,0:T(8,128)S(1)}) custom-call(f32[16,4,128]{2,1,0:T(4,128)S(1)} %get-tuple-element.55.target, s32[144]{0:T(256)S(1)} %get-tuple-element.39.table, f32[3,7,4,128]{3,2,1,0:T(4,128)S(1)} %collective-permute-done.4.from_even, ...), custom_call_target="tpu_custom_call", output_to_operand_aliasing={{0}: (4, {}), {1}: (5, {})} | custom-call | bytes 12000000 | tf_op jit(solution)/shard_map/near/pallas_call | solution.py:441
  61.9 0.0 collective-permute-done.6.from_even
  61.9 0.5 collective-permute-done.7.from_odd
  62.4 7.3 %far.3 = (f32[16,48,8,128]{3,2,1,0:T(8,128)S(1)}, f32[16,8,128]{2,1,0:T(8,128)S(1)}, f32[16,6144]{1,0:T(8,128)S(1)}, f32[128,2,128]{2,1,0:T(2,128)S(1)}) custom-call(f32[16,4,128]{2,1,0:T(4,128)S(1)} %get-tuple-element.55.target, s32[144]{0:T(256)S(1)} %get-tuple-element.39.table, ...), custom_call_target="tpu_custom_call", output_to_operand_aliasing={{0}: (4, {}), {1}: (5, {})} | custom-call | bytes 36000000 | tf_op jit(solution)/shard_map/far/pallas_call | solution.py:455
  69.7 17.6 %all_to_all.11.sums = f32[128,2,128]{2,1,0:T(2,128)S(1)} all-to-all(f32[128,2,128]{2,1,0:T(2,128)S(1)} %get-tuple-element.68), channel_id=1, replica_groups=mesh['sky'=16,'depth'=8] {'sky','depth'}, dimensions={0} | all-to-all | bytes 262144 | tf_op jit(solution)/shard_map/all_to_all | solution.py:505
  87.3 1.0 %last.1 = f32[3,16,128]{2,1,0:T(8,128)} custom-call(f32[128,2,128]{2,1,0:T(2,128)S(1)} %all_to_all.11.sums, f32[16,6144]{1,0:T(8,128)S(1)} %get-tuple-element.69.grad, f32[16,4,128]{2,1,0:T(4,128)S(1)} %get-tuple-element.70.travel, f32[16,128]{1,0:T(8,128)S(1)} %get-tuple-element.54.logs), custom_call_target="tpu_custom_call" | custom-call | tf_op jit(solution)/shard_map/last/pallas_call | solution.py:507
  (7 shorter events, 0.1 us)
Async XLA Ops:
  1.9 12.0 %collective-permute-start = (f32[3,7,4,128]{3,2,1,0:T(4,128)S(1)}, f32[3,7,4,128]{3,2,1,0:T(4,128)S(1)}, u32[]{:S(2)}, u32[]{:S(2)}) collective-permute-start(f32[3,7,4,128]{3,2,1,0:T(4,128)S(1)} %get-tuple-element.41), channel_id=1, source_target_pairs={{0,8},{8,0},{16,24},{24,16},{32,40},{40,32},{48,56},{56,48},{64,72... | collective-permute-start | bytes 129032 | tf_op jit(solution)/shard_map/ppermute | solution.py:402
  4.5 9.5 %collective-permute-start.1 = (f32[3,7,4,128]{3,2,1,0:T(4,128)S(1)}, f32[3,7,4,128]{3,2,1,0:T(4,128)S(1)}, u32[]{:S(2)}, u32[]{:S(2)}) collective-permute-start(f32[3,7,4,128]{3,2,1,0:T(4,128)S(1)} %get-tuple-element.42), channel_id=1, source_target_pairs={{8,16},{16,8},{24,32},{32,24},{40,48},{48,40},{56,64},{64,56},{72,... | collective-permute-start | bytes 129032 | tf_op jit(solution)/shard_map/ppermute | solution.py:402
  14.0 8.0 %collective-permute-start.2 = (f32[3,7,4,128]{3,2,1,0:T(4,128)S(1)}, f32[3,7,4,128]{3,2,1,0:T(4,128)S(1)}, u32[]{:S(2)}, u32[]{:S(2)}) collective-permute-start(f32[3,7,4,128]{3,2,1,0:T(4,128)S(1)} %pad_maximum_fusion), channel_id=1, source_target_pairs={{0,1},{1,0},{2,3},{3,2},{4,5},{5,4},{6,7},{7,6},{8,9},{9,8},{10,11... | collective-permute-start | bytes 129032 | tf_op jit(solution)/shard_map/ppermute | solution.py:402
  16.2 5.8 %collective-permute-start.3 = (f32[3,7,4,128]{3,2,1,0:T(4,128)S(1)}, f32[3,7,4,128]{3,2,1,0:T(4,128)S(1)}, u32[]{:S(2)}, u32[]{:S(2)}) collective-permute-start(f32[3,7,4,128]{3,2,1,0:T(4,128)S(1)} %pad_maximum_fusion.1), channel_id=1, source_target_pairs={{1,2},{2,1},{3,4},{4,3},{5,6},{6,5},{9,10},{10,9},{11,12},{12,11},... | collective-permute-start | bytes 129032 | tf_op jit(solution)/shard_map/ppermute | solution.py:402
  47.7 7.4 %collective-permute-start.4 = (f32[3,7,4,128]{3,2,1,0:T(4,128)S(1)}, f32[3,7,4,128]{3,2,1,0:T(4,128)S(1)}, u32[]{:S(2)}, u32[]{:S(2)}) collective-permute-start(f32[3,7,4,128]{3,2,1,0:T(4,128)S(1)} %get-tuple-element.57), channel_id=1, source_target_pairs={{0,8},{8,0},{16,24},{24,16},{32,40},{40,32},{48,56},{56,48},{64,72... | collective-permute-start | bytes 129032 | tf_op jit(solution)/shard_map/ppermute | solution.py:402
  48.1 7.0 %collective-permute-start.5 = (f32[3,7,4,128]{3,2,1,0:T(4,128)S(1)}, f32[3,7,4,128]{3,2,1,0:T(4,128)S(1)}, u32[]{:S(2)}, u32[]{:S(2)}) collective-permute-start(f32[3,7,4,128]{3,2,1,0:T(4,128)S(1)} %get-tuple-element.58), channel_id=1, source_target_pairs={{8,16},{16,8},{24,32},{32,24},{40,48},{48,40},{56,64},{64,56},{72,... | collective-permute-start | bytes 129032 | tf_op jit(solution)/shard_map/ppermute | solution.py:402
  55.1 6.8 %collective-permute-start.6 = (f32[3,7,4,128]{3,2,1,0:T(4,128)S(1)}, f32[3,7,4,128]{3,2,1,0:T(4,128)S(1)}, u32[]{:S(2)}, u32[]{:S(2)}) collective-permute-start(f32[3,7,4,128]{3,2,1,0:T(4,128)S(1)} %pad_maximum_fusion.2), channel_id=1, source_target_pairs={{0,1},{1,0},{2,3},{3,2},{4,5},{5,4},{6,7},{7,6},{8,9},{9,8},{10,11... | collective-permute-start | bytes 129032 | tf_op jit(solution)/shard_map/ppermute | solution.py:402
  57.1 5.3 %collective-permute-start.7 = (f32[3,7,4,128]{3,2,1,0:T(4,128)S(1)}, f32[3,7,4,128]{3,2,1,0:T(4,128)S(1)}, u32[]{:S(2)}, u32[]{:S(2)}) collective-permute-start(f32[3,7,4,128]{3,2,1,0:T(4,128)S(1)} %pad_maximum_fusion.3), channel_id=1, source_target_pairs={{1,2},{2,1},{3,4},{4,3},{5,6},{6,5},{9,10},{10,9},{11,12},{12,11},... | collective-permute-start | bytes 129032 | tf_op jit(solution)/shard_map/ppermute | solution.py:402
